TPU v7x, 128 devices: a whole 4x4x4 slice. The times are simulated.
128 devices in a mesh: member: 32 (over x, z, core), mp: 4 (over y).
Axes of the slice: x: 4, y: 4, z: 4, core: 2. Of those that a mesh axis runs over, the one named last changes fastest.
Arguments:
- latents: bfloat16 [128, 1024, 1024], P('member', 'mp'), may hold values from -6 to 6
- w_first: bfloat16 [1024, 2048], P(None, 'mp'), may hold values from -0.1875 to 0.1875
- w_second: bfloat16 [2048, 1024], P('mp'), may hold values from -0.125 to 0.125
- readout_matrix: bfloat16 [1024, 768], P(None, 'mp'), may hold values from -0.1875 to 0.1875
- observed: float32 [1024, 768], P(('mp', 'member')), may hold values from -9 to 9
- obs_index: int32 [1024], P(('mp', 'member')), may hold values from 0 to 1023, as said below
- valid_mask: int32 [1024], P(('mp', 'member')), may hold values from 0 to 1
Outputs:
- grad_first: float32 [1024, 2048], P(('member', 'mp'))
- grad_second: float32 [2048, 1024], P(('member', 'mp'))
- grad_head: float32 [1024, 768], P(('member', 'mp'))
- loss: float32 [], replicated
Inputs may be any that keep to these rules, and one draw needn't show every extreme that they name: obs_index[p] names a record of the same aligned block of 8 patches as p.
All inputs are finite; a program needn't handle non-finite values.
Results may differ from a plain program's by a relative error of at most 0.006.
Values may be sent and summed in bfloat16 or wider, within the bound.
No kernel may reach another device: no remote copies, remote signals or barrier semaphores. Data moves between devices by JAX's collectives and lax.ppermute only.
A program may use at most 128 MiB of HBM per device.

v0:
```python
import jax
import jax.numpy as jnp
from jax import lax
from jax.sharding import PartitionSpec as P

SMOOTHING = 1.0
LOSS_SCALE = 4096.0


def split_up(x, dim, devices):
    lengths = x.shape
    parts = x.reshape(*lengths[:dim], devices, lengths[dim] // devices, *lengths[dim + 1 :])
    return jnp.moveaxis(parts, dim, 0)


def sent_and_summed(x, axis, dim):
    parts = split_up(x, dim, lax.axis_size(axis))
    arrived = lax.all_to_all(parts, axis, split_axis=0, concat_axis=0, tiled=True)
    return arrived.sum(axis=0)


def in_order(parts, dim):
    parts = jnp.moveaxis(parts, 0, dim)
    lengths = parts.shape
    return parts.reshape(*lengths[:dim], lengths[dim] * lengths[dim + 1], *lengths[dim + 2 :])


def one_gather(arrays, axis, dims):
    vector = jnp.concatenate([a.reshape(-1) for a in arrays])
    lines, at, outs = (lax.all_gather(vector, axis), 0, [])
    for a, dim in zip(arrays, dims):
        parts = lines[:, at : at + a.size].reshape(-1, *a.shape)
        outs.append(in_order(parts, dim))
        at += a.size
    return tuple(outs)


def gelu_fn(values):
    return jax.nn.gelu(values, approximate=True)


def gelu_back(preact, upstream):
    return jax.vjp(gelu_fn, preact)[1](upstream)[0]


def row_outer(left_rows, right_rows):
    return lax.dot_general(
        left_rows, right_rows, (((0,), (0,)), ((), ())), preferred_element_type=jnp.float32
    )


def weight_sum(left_rows, right_rows):
    across = lax.axis_size("member")
    within = lax.axis_size("mp")
    share_rows = left_rows.shape[1] // (across * within)
    local_grad = row_outer(left_rows, right_rows)
    reordered = (
        local_grad.reshape(across, within, share_rows, -1)
        .transpose(1, 0, 2, 3)
        .reshape(left_rows.shape[1], -1)
    )
    group_sum = lax.psum_scatter(reordered, "mp", scatter_dimension=0, tiled=True)
    return sent_and_summed(group_sum, "member", 0)


def per_device(latents, w_first, w_second, readout_matrix, observed, obs_index, valid_mask):
    sample_portion, tile_portion, feature_width = latents.shape
    full_first, full_second, complete_head = one_gather(
        (w_first, w_second, readout_matrix), "mp", (1, 0, 1)
    )
    token_rows = latents.reshape(sample_portion * tile_portion, feature_width)
    preact = jnp.dot(token_rows, full_first, preferred_element_type=jnp.float32)
    hidden = gelu_fn(preact).astype(jnp.bfloat16)
    skip_activation = (
        token_rows.astype(jnp.float32)
        + jnp.dot(hidden, full_second, preferred_element_type=jnp.float32)
    ).astype(jnp.bfloat16)
    prediction_lines = jnp.dot(
        skip_activation, complete_head, preferred_element_type=jnp.float32
    ).astype(jnp.bfloat16)
    prediction_lines = prediction_lines.reshape(sample_portion, tile_portion, -1)
    ensemble_reduced = lax.all_to_all(
        prediction_lines, "member", split_axis=1, concat_axis=0, tiled=True
    )
    sample_indices = ensemble_reduced.shape[0]
    owned_count = ensemble_reduced.shape[1]
    offset_row = (
        lax.axis_index("mp") * lax.axis_size("member") + lax.axis_index("member")
    ) * owned_count
    target = jnp.take(observed, obs_index - offset_row, axis=0)
    predicted_samples = ensemble_reduced.astype(jnp.float32)
    gram_matrix = jnp.einsum(
        "mpo,npo->pmn", ensemble_reduced, ensemble_reduced, preferred_element_type=jnp.float32
    )
    squares = jnp.sum(predicted_samples * predicted_samples, axis=2).T
    dist_sq = squares[:, :, None] + squares[:, None, :] - 2.0 * gram_matrix
    spread = jnp.sqrt(dist_sq + SMOOTHING)
    kernel = 1.0 / spread
    kernel_sum = jnp.sum(kernel, axis=2)
    pulled = jnp.einsum("pmn,npo->mpo", kernel, predicted_samples, precision=lax.Precision.HIGHEST)
    offset = predicted_samples - target[None]
    error_norm = jnp.sqrt(jnp.sum(offset * offset, axis=2) + SMOOTHING)
    repulse = predicted_samples * kernel_sum.T[:, :, None] - pulled
    validity = valid_mask.astype(jnp.float32)
    grad_raw = (
        LOSS_SCALE
        * validity[None, :, None]
        * (
            offset / (sample_indices * error_norm[:, :, None])
            - repulse / (sample_indices * sample_indices)
        )
    ).astype(jnp.bfloat16)
    scores = validity * (
        jnp.mean(error_norm, axis=0)
        - jnp.sum(spread, axis=(1, 2)) / (2.0 * sample_indices * sample_indices)
    )
    score_part = jnp.sum(scores)
    count_part = jnp.sum(validity)
    valid_count = lax.psum(count_part, ("member", "mp"))
    returned = lax.all_to_all(grad_raw, "member", split_axis=0, concat_axis=1, tiled=True)
    grad_rows = returned.reshape(sample_portion * tile_portion, -1)
    resid_grad = jnp.dot(grad_rows, complete_head.T, preferred_element_type=jnp.float32).astype(
        jnp.bfloat16
    )
    hidden_grad = jnp.dot(resid_grad, full_second.T, preferred_element_type=jnp.float32)
    preact_grad = gelu_back(preact, hidden_grad).astype(jnp.bfloat16)
    sum_first = weight_sum(token_rows, preact_grad)
    sum_second = weight_sum(hidden, resid_grad)
    sum_head = weight_sum(skip_activation, grad_rows)
    score_total = lax.psum(score_part, ("member", "mp"))
    valid_total = jnp.maximum(valid_count, 1.0)
    grad_scale = 1.0 / valid_total
    return (
        sum_first * grad_scale,
        sum_second * grad_scale,
        sum_head * grad_scale,
        score_total / valid_total,
    )


def solution(mesh):
    return jax.shard_map(
        per_device,
        mesh=mesh,
        in_specs=(
            P("member", "mp", None),
            P(None, "mp"),
            P("mp", None),
            P(None, "mp"),
            P(("mp", "member"), None),
            P(("mp", "member")),
            P(("mp", "member")),
        ),
        out_specs=(
            P(("member", "mp"), None),
            P(("member", "mp"), None),
            P(("member", "mp"), None),
            P(),
        ),
        check_vma=False,
    )
```

profile of v0, /device:TPU:1, one launch (start us, length us, event | category | flops | bytes accessed | tf_op | source)
XLA Modules:
  0.0 563.1 jit_solution(6890008387283289417)
XLA Ops:
  11.1 14.1 %pad_maximum_fusion = bf16[1245184]{0:T(1024)(128)(2,1)} fusion(bf16[196608]{0:T(1024)(128)(2,1)S(1)} %reshape.107, bf16[524288]{0:T(1024)(128)(2,1)S(1)} %bitcast.110, bf16[524288]{0:T(1024)(128)(2,1)S(1)} %bitcast.109), kind=kLoop, calls=%fused_computation.31 | loop fusion | flops 7471104 | bytes 4980736 | tf_op jit(solution)/shard_map/concatenate | solution.py:29
  25.2 2.6 copy.100
  27.8 97.2 %all-gather.3.cloned.1.call-done = bf16[4980736]{0:T(1024)(128)(2,1)} async-done(((bf16[1245184]{0:T(1024)(128)(2,1)}), bf16[4980736]{0:T(1024)(128)(2,1)}) %all-gather.3.cloned.1.call-update) | async-done | bytes 9961488 | tf_op jit(solution)/shard_map/all_gather | solution.py:30
  125.0 13.0 %reshape.130 = bf16[4,1245184]{1,0:T(4,128)(2,1)} reshape(bf16[4980736]{0:T(1024)(128)(2,1)} %all-gather.3.cloned.1.call-done) | data formatting | bytes 19922944 | tf_op jit(solution)/shard_map/all_gather | solution.py:30
  137.9 8.3 %fusion.38 = (bf16[4,524288]{1,0:T(4,128)(2,1)}, bf16[4,524288]{1,0:T(4,128)(2,1)}) fusion(bf16[4,1245184]{1,0:T(4,128)(2,1)} %reshape.130), kind=kLoop, calls=%fused_computation.64 | loop fusion | bytes 16777216 | tf_op jit(solution)/shard_map/slice | solution.py:32
  146.3 8.0 %reshape_reshape.3 = bf16[2048,1024]{1,0:T(8,128)(2,1)} reshape(bf16[4,524288]{1,0:T(4,128)(2,1)} %get-tuple-element.14) | data formatting | bytes 8388608 | tf_op jit(solution)/shard_map/reshape;reshape | solution.py:25
  154.3 5.0 copy.110
  159.3 6.4 %copy.75 = bf16[1024,4,512]{0,2,1:T(8,128)(2,1)} copy(bf16[1024,4,512]{2,0,1:T(8,128)(2,1)} %bitcast.101) | data formatting | bytes 8388608 | tf_op jit(solution)/shard_map/transpose | solution.py:23
  165.7 2.8 reshape.133
  168.4 3.1 reshape.110
  171.5 2.4 copy.76
  173.9 7.1 %fusion.41 = f32[2048,1024]{1,0:T(8,128)S(1)} fusion(bf16[1024,2048]{0,1:T(8,128)(2,1)} %bitcast.111, bf16[1024,1024]{1,0:T(8,128)(2,1)} %bitcast.112), kind=kOutput, calls=%fused_computation.66 | convolution fusion | flops 4294967296 | bytes 14680064 | tf_op jit(solution)/shard_map/dot_general | solution.py:72
  181.1 5.2 add_convert_fusion
  186.4 1.9 convolution_convert_fusion.1
  188.3 2.4 copy.77
  190.6 7.7 %all-to-all-start = ((bf16[4,256,768]{2,0,1:T(4,128)(2,1)}), bf16[4,256,768]{2,0,1:T(4,128)(2,1)S(1)}, u32[]{:S(2)}, u32[]{:S(2)}) async-start(bf16[4,256,768]{2,0,1:T(4,128)(2,1)} %copy.77), calls=%async_computation | async-start | bytes 3145728 | tf_op jit(solution)/shard_map/all_to_all | solution.py:82
  199.1 21.9 %all-to-all-done = bf16[4,256,768]{2,0,1:T(4,128)(2,1)S(1)} async-done(((bf16[4,256,768]{2,0,1:T(4,128)(2,1)}), bf16[4,256,768]{2,0,1:T(4,128)(2,1)S(1)}, u32[]{:S(2)}, u32[]{:S(2)}) %all-to-all-start) | async-done | bytes 1572896 | tf_op jit(solution)/shard_map/all_to_all | solution.py:82
  225.8 2.5 fusion.20
  229.3 26.9 %all_to_all.48 = bf16[128,8,768]{2,1,0:T(8,128)(2,1)S(1)} all-to-all(bf16[128,8,768]{2,1,0:T(8,128)(2,1)S(1)} %copy.88), channel_id=1, replica_groups=mesh['member'=32,'mp'=4] {'member'}, dimensions={0} | all-to-all | bytes 3145728 | tf_op jit(solution)/shard_map/all_to_all | solution.py:120
  256.3 1.8 convolution_bitcast_fusion
  258.1 2.0 copy.94
  260.2 1.8 convolution_convert_fusion
  262.0 8.3 %fusion.34 = f32[2048,1024]{1,0:T(8,128)S(1)} fusion(bf16[1024,1024]{1,0:T(8,128)(2,1)S(1)} %convolution_convert_fusion, f32[2048,1024]{1,0:T(8,128)} %copy-done.14), kind=kOutput, calls=%fused_computation.62 | convolution fusion | flops 4313841664 | bytes 18874368 | tf_op jit(solution)/shard_map/dot_general | solution.py:47
  270.3 4.1 copy.93
  276.0 16.7 %fusion.10 = f32[2048,1024]{0,1:T(8,128)} fusion(bf16[1024,1024]{1,0:T(8,128)(2,1)S(1)} %bitcast.114, f32[2048,1024]{1,0:T(8,128)} %copy-done.14, bf16[1024,1024]{1,0:T(8,128)(2,1)} %copy-done.13, bf16[2048,1024]{1,0:T(8,128)(2,1)} %reshape_reshape.3), kind=kOutput, calls=%fused_computation.17 | convolution fusion | flops 8631877632 | bytes 25165824 | tf_op jit(solution)/shard_map/dot_general | solution.py:47
  292.7 7.8 %copy.92 = f32[32,4,8,2048]{3,2,0,1:T(8,128)} copy(f32[32,4,8,2048]{3,2,1,0:T(8,128)} %bitcast.106) | data formatting | bytes 16777216 | tf_op jit(solution)/shard_map/reshape | solution.py:58
  300.5 17.8 %all_to_all.49 = f32[32,8,768]{2,1,0:T(8,128)S(1)} all-to-all(f32[32,8,768]{2,1,0:T(8,128)} %bitcast.124), channel_id=1, replica_groups=mesh['member'=32,'mp'=4] {'member'}, dimensions={0} | all-to-all | bytes 1572864 | tf_op jit(solution)/shard_map/all_to_all | solution.py:18
  318.4 59.9 %reduce-scatter.6.cloned.1.call-done = f32[512,1024]{1,0:T(8,128)} async-done(((f32[2048,1024]{1,0:T(8,128)}), f32[512,1024]{1,0:T(8,128)}) %reduce-scatter.6.cloned.1.call-update) | async-done | bytes 2097168 | tf_op jit(solution)/shard_map/reduce_scatter | solution.py:62
  378.3 7.6 %all-to-all-start.3 = ((f32[32,16,1024]{2,1,0:T(8,128)}), f32[32,16,1024]{2,1,0:T(8,128)S(1)}, u32[]{:S(2)}, u32[]{:S(2)}) async-start(f32[32,16,1024]{2,1,0:T(8,128)} %bitcast.116), calls=%async_computation.5 | async-start | bytes 4194304 | tf_op jit(solution)/shard_map/all_to_all | solution.py:18
  385.9 75.0 %reduce-scatter.4.cloned.1.call-done = f32[256,2048]{1,0:T(8,128)} async-done(((f32[1024,2048]{1,0:T(8,128)}), f32[256,2048]{1,0:T(8,128)}) %reduce-scatter.4.cloned.1.call-update) | async-done | bytes 2097168 | tf_op jit(solution)/shard_map/reduce_scatter | solution.py:62
  460.9 7.8 %all-to-all-start.2 = ((f32[32,8,2048]{2,1,0:T(8,128)}), f32[32,8,2048]{2,1,0:T(8,128)}, u32[]{:S(2)}, u32[]{:S(2)}) async-start(f32[32,8,2048]{2,1,0:T(8,128)} %bitcast.115), calls=%async_computation.3 | async-start | bytes 4194304 | tf_op jit(solution)/shard_map/all_to_all | solution.py:18
  468.7 81.5 %all-reduce = (f32[]{:T(128)}, f32[]{:T(128)}) all-reduce(f32[]{:T(128)} %get-tuple-element.9, f32[]{:T(128)} %get-tuple-element.8), channel_id=1, replica_groups=mesh['member'=32,'mp'=4] {'member','mp'}, use_global_device_ids=true, to_apply=%region_6.7 | all-reduce | flops 2 | bytes 16 | tf_op jit(solution)/shard_map/psum | solution.py:119
  (70 shorter events, 15.9 us)
Async XLA Ops:
  7.2 191.2 %copy-start = (f32[8,768]{1,0:T(8,128)S(1)}, f32[8,768]{1,0:T(8,128)}, u32[]{:S(2)}) copy-start(f32[8,768]{1,0:T(8,128)} %param.11) | copy-start | bytes 73732
  7.2 3.6 copy-start.8
  7.2 117.8 %all-gather.3.cloned.1.call-start = ((), (), s32[]{:S(2)}) async-start(), calls=%async_computation.11 | async-start | bytes 12451840 | tf_op jit(solution)/shard_map/all_gather | solution.py:30
  11.1 14.1 %copy-start.3 = (bf16[4,256,1024]{2,1,0:T(8,128)(2,1)S(1)}, bf16[4,256,1024]{2,1,0:T(8,128)(2,1)}, u32[]{:S(2)}) copy-start(bf16[4,256,1024]{2,1,0:T(8,128)(2,1)} %param.7) | copy-start | bytes 6291460
  159.3 6.4 %slice-start = ((bf16[4,1245184]{1,0:T(4,128)(2,1)}), bf16[4,196608]{1,0:T(4,128)(2,1)S(1)}, s32[]{:S(2)}) async-start(bf16[4,1245184]{1,0:T(4,128)(2,1)} %reshape.130), calls=%async_computation.12 | async-start | bytes 3145728 | tf_op jit(solution)/shard_map/slice | solution.py:32
  173.9 7.1 %copy-start.2 = (bf16[2048,1024]{1,0:T(8,128)(2,1)S(1)}, bf16[2048,1024]{1,0:T(8,128)(2,1)}, u32[]{:S(2)}) copy-start(bf16[2048,1024]{1,0:T(8,128)(2,1)} %reshape_reshape.3) | copy-start | bytes 12582916
  173.9 7.2 %copy-start.5 = (bf16[1024,1024]{0,1:T(8,128)(2,1)S(1)}, bf16[1024,1024]{0,1:T(8,128)(2,1)}, u32[]{:S(2)}) copy-start(bf16[1024,1024]{0,1:T(8,128)(2,1)} %copy.100) | copy-start | bytes 6291460
  181.1 5.2 copy-start.14
  181.1 5.3 copy-start.6
  186.4 1.9 copy-start.11
  188.3 10.1 %copy-start.9 = (s32[8]{0:T(128)S(1)}, s32[8]{0:T(128)}, u32[]{:S(2)}) copy-start(s32[8]{0:T(128)} %param.12) | copy-start | bytes 100
  190.6 30.4 %all-to-all-start = ((bf16[4,256,768]{2,0,1:T(4,128)(2,1)}), bf16[4,256,768]{2,0,1:T(4,128)(2,1)S(1)}, u32[]{:S(2)}, u32[]{:S(2)}) async-start(bf16[4,256,768]{2,0,1:T(4,128)(2,1)} %copy.77), calls=%async_computation | async-start | bytes 3145728 | tf_op jit(solution)/shard_map/all_to_all | solution.py:82
  198.3 102.2 %reduce-scatter.8.cloned.1.call-start = ((), (), s32[]{:S(2)}) async-start(), calls=%async_computation.10 | async-start | bytes 3932160 | tf_op jit(solution)/shard_map/reduce_scatter | solution.py:62
  224.1 1.2 copy-start.10
  228.4 27.9 %copy-start.12 = (bf16[1024,1024]{0,1:T(8,128)(2,1)S(1)}, bf16[1024,1024]{0,1:T(8,128)(2,1)}, u32[]{:S(2)}) copy-start(bf16[1024,1024]{0,1:T(8,128)(2,1)} %copy-done.11) | copy-start | bytes 6291460
  258.1 2.1 copy-start.7
  260.1 118.1 %reduce-scatter.6.cloned.1.call-start = ((), (), s32[]{:S(2)}) async-start(), calls=%async_computation.9 | async-start | bytes 10485760 | tf_op jit(solution)/shard_map/reduce_scatter | solution.py:62
  262.0 8.3 %copy-start.13 = (bf16[1024,1024]{1,0:T(8,128)(2,1)}, bf16[1024,1024]{1,0:T(8,128)(2,1)S(1)}, u32[]{:S(2)}) copy-start(bf16[1024,1024]{1,0:T(8,128)(2,1)S(1)} %convolution_convert_fusion) | copy-start | bytes 6291460
  274.4 1.6 copy-start.4
  274.4 186.5 %reduce-scatter.4.cloned.1.call-start = ((), (), s32[]{:S(2)}) async-start(), calls=%async_computation.8 | async-start | bytes 10485760 | tf_op jit(solution)/shard_map/reduce_scatter | solution.py:62
  378.3 82.6 %all-to-all-start.3 = ((f32[32,16,1024]{2,1,0:T(8,128)}), f32[32,16,1024]{2,1,0:T(8,128)S(1)}, u32[]{:S(2)}, u32[]{:S(2)}) async-start(f32[32,16,1024]{2,1,0:T(8,128)} %bitcast.116), calls=%async_computation.5 | async-start | bytes 4194304 | tf_op jit(solution)/shard_map/all_to_all | solution.py:18
  460.9 94.4 %copy-start.1 = (f32[8,768]{1,0:T(8,128)S(1)}, f32[8,768]{1,0:T(8,128)}, u32[]{:S(2)}) copy-start(f32[8,768]{1,0:T(8,128)} %param.11) | copy-start | bytes 73732
  460.9 92.0 %all-to-all-start.2 = ((f32[32,8,2048]{2,1,0:T(8,128)}), f32[32,8,2048]{2,1,0:T(8,128)}, u32[]{:S(2)}, u32[]{:S(2)}) async-start(f32[32,8,2048]{2,1,0:T(8,128)} %bitcast.115), calls=%async_computation.3 | async-start | bytes 4194304 | tf_op jit(solution)/shard_map/all_to_all | solution.py:18
Sparse Core Ops, SparseCore 0:
  25.3 99.6 all-gather.2
  260.3 35.2 reduce-scatter.7
  298.0 80.2 reduce-scatter.5
  380.6 80.2 reduce-scatter.3
where the time goes:
time: 573 us; the launch traced here: 563 us
  waiting for transfers between devices  254 us (44%)
  blocking collectives  126 us (22%)
  local copies, waits for them, and re-layouts  76.1 us (13%)
  matrix products  46 us (8%)
  starting transfers between devices  23.4 us (4%)
  other arithmetic  20.4 us (4%)
  between operations  16.8 us (3%)
    reduce_scatter x3, waiting for transfers between devices, weight_sum(): lax.psum_scatter(reordered, 'mp', scatter_dimension=0, tiled=True)  135 us
    all_gather x1, waiting for transfers between devices, one_gather(): lines, at, outs = (lax.all_gather(vector, axis), 0, [])  97.2 us
    psum x1, blocking collectives, per_device(): valid_count = lax.psum(count_part, ('member', 'mp'))  81.5 us
    all_to_all x1, blocking collectives, per_device(): lax.all_to_all(grad_raw, 'member', split_axis=0, concat_axis=1, tiled=True)  26.9 us
    dot_general x3, matrix products, row_outer(): lax.dot_general(left_rows, right_rows, (((0,), (0,)), ((), ())), preferre...  26.8 us
    all_to_all x1, waiting for transfers between devices, per_device(): lax.all_to_all(prediction_lines, 'member', split_axis=1, concat_axis=0, t...  21.9 us
    all_to_all x1, blocking collectives, sent_and_summed(): lax.all_to_all(parts, axis, split_axis=0, concat_axis=0, tiled=True)  17.8 us
    all_to_all x2, starting transfers between devices, sent_and_summed(): lax.all_to_all(parts, axis, split_axis=0, concat_axis=0, tiled=True)  15.4 us
  transfers between devices with their start and end apart: 7, of which 4 were waited for; matrix products, arithmetic and copies ran while one was open for 8% of the time, Pallas kernels for 0%

commit v1 on v0

--- a/solution.py
+++ b/solution.py
@@ -79,8 +79,14 @@
         skip_activation, complete_head, preferred_element_type=jnp.float32
     ).astype(jnp.bfloat16)
     prediction_lines = prediction_lines.reshape(sample_portion, tile_portion, -1)
-    ensemble_reduced = lax.all_to_all(
-        prediction_lines, "member", split_axis=1, concat_axis=0, tiled=True
+    ensemble_reduced = jnp.concatenate(
+        lax.all_to_all(
+            jnp.stack(jnp.split(prediction_lines, lax.psum(1, axis_name="member"), axis=1)),
+            axis_name="member",
+            split_axis=0,
+            concat_axis=0,
+        ),
+        axis=0,
     )
     sample_indices = ensemble_reduced.shape[0]
     owned_count = ensemble_reduced.shape[1]

time: 573 us -> 588 us (1.026)
  local copies, waits for them, and re-layouts: 76.1 us -> 94.3 us
    unnamed x35 -> x66, local copies, waits for them, and re-layouts: 12.4 us -> 33.6 us
  transfers between devices with their start and end apart: 7 -> 7, of which waited for: 4 -> 4; matrix products, arithmetic and copies ran while one was open for 8% -> 7% of each run, Pallas kernels for 0% -> 0%
where the time goes in v1:
time: 588 us; the launch traced here: 579 us
  waiting for transfers between devices  252 us (43%)
  blocking collectives  126 us (21%)
  local copies, waits for them, and re-layouts  94.3 us (16%)
  matrix products  46.5 us (8%)
  starting transfers between devices  23.3 us (4%)
  other arithmetic  19.4 us (3%)
  between operations  17 us (3%)
    reduce_scatter x3, waiting for transfers between devices, weight_sum(): lax.psum_scatter(reordered, 'mp', scatter_dimension=0, tiled=True)  135 us
    all_gather x1, waiting for transfers between devices, one_gather(): lines, at, outs = (lax.all_gather(vector, axis), 0, [])  95.7 us
    psum x1, blocking collectives, per_device(): valid_count = lax.psum(count_part, ('member', 'mp'))  81.5 us
    unnamed x66, local copies, waits for them, and re-layouts  33.6 us
    dot_general x3, matrix products, row_outer(): lax.dot_general(left_rows, right_rows, (((0,), (0,)), ((), ())), preferre...  26.8 us
    all_to_all x1, blocking collectives, per_device(): lax.all_to_all(grad_raw, 'member', split_axis=0, concat_axis=1, tiled=True)  26.5 us
    all_to_all x1, waiting for transfers between devices, per_device(): lax.all_to_all(jnp.stack(jnp.split(prediction_lines, lax.psum(1, axis_nam...  21.9 us
    all_to_all x1, blocking collectives, sent_and_summed(): lax.all_to_all(parts, axis, split_axis=0, concat_axis=0, tiled=True)  17.8 us
  transfers between devices with their start and end apart: 7, of which 4 were waited for; matrix products, arithmetic and copies ran while one was open for 7% of the time, Pallas kernels for 0%

profile of v1, /device:TPU:1, one launch (start us, length us, event | category | flops | bytes accessed | tf_op | source)
XLA Modules:
  0.0 578.7 jit_solution(612849403256102766)
XLA Ops:
  9.9 14.1 %pad_maximum_fusion = bf16[1245184]{0:T(1024)(128)(2,1)} fusion(bf16[196608]{0:T(1024)(128)(2,1)S(1)} %reshape.110, bf16[524288]{0:T(1024)(128)(2,1)S(1)} %bitcast.226, bf16[524288]{0:T(1024)(128)(2,1)S(1)} %bitcast.225), kind=kLoop, calls=%fused_computation.31 | loop fusion | flops 7471104 | bytes 4980736 | tf_op jit(solution)/shard_map/concatenate | solution.py:29
  25.6 2.6 copy.75
  28.1 95.7 %all-gather.3.cloned.1.call-done = bf16[4980736]{0:T(1024)(128)(2,1)} async-done(((bf16[1245184]{0:T(1024)(128)(2,1)}), bf16[4980736]{0:T(1024)(128)(2,1)}) %all-gather.3.cloned.1.call-update) | async-done | bytes 9961488 | tf_op jit(solution)/shard_map/all_gather | solution.py:30
  123.8 13.0 %reshape.134 = bf16[4,1245184]{1,0:T(4,128)(2,1)} reshape(bf16[4980736]{0:T(1024)(128)(2,1)} %all-gather.3.cloned.1.call-done) | data formatting | bytes 19922944 | tf_op jit(solution)/shard_map/all_gather | solution.py:30
  136.8 8.6 %fusion.50 = (bf16[4,524288]{1,0:T(4,128)(2,1)}, bf16[4,524288]{1,0:T(4,128)(2,1)}) fusion(bf16[4,1245184]{1,0:T(4,128)(2,1)} %reshape.134), kind=kLoop, calls=%fused_computation.130 | loop fusion | bytes 16777216 | tf_op jit(solution)/shard_map/slice | solution.py:32
  145.4 8.0 %reshape_reshape.3 = bf16[2048,1024]{1,0:T(8,128)(2,1)} reshape(bf16[4,524288]{1,0:T(4,128)(2,1)} %get-tuple-element.14) | data formatting | bytes 8388608 | tf_op jit(solution)/shard_map/reshape;reshape | solution.py:25
  153.4 5.0 copy.97
  158.4 6.4 %copy.54 = bf16[1024,4,512]{0,2,1:T(8,128)(2,1)} copy(bf16[1024,4,512]{2,0,1:T(8,128)(2,1)} %bitcast.216) | data formatting | bytes 8388608 | tf_op jit(solution)/shard_map/transpose | solution.py:23
  164.8 2.8 reshape.137
  167.6 3.1 reshape.113
  170.7 2.4 copy.55
  173.1 7.1 %fusion.53 = f32[2048,1024]{1,0:T(8,128)S(1)} fusion(bf16[1024,2048]{0,1:T(8,128)(2,1)} %bitcast.227, bf16[1024,1024]{1,0:T(8,128)(2,1)} %bitcast.228), kind=kOutput, calls=%fused_computation.132 | convolution fusion | flops 4294967296 | bytes 14680064 | tf_op jit(solution)/shard_map/dot_general | solution.py:72
  180.3 5.2 add_convert_fusion
  185.5 1.9 convolution_convert_fusion.1
  207.2 7.7 %all-to-all-start = ((bf16[32,4,8,768]{3,2,1,0:T(8,128)(2,1)}), bf16[32,4,8,768]{3,2,1,0:T(8,128)(2,1)S(1)}, u32[]{:S(2)}, u32[]{:S(2)}) async-start(bf16[32,4,8,768]{3,2,1,0:T(8,128)(2,1)} %constant_dynamic-update-slice_fusion), calls=%async_computation | async-start | bytes 3145728 | tf_op jit(solution)/shard_map/all_to_all | solution.py:83
  215.6 21.9 %all-to-all-done = bf16[32,4,8,768]{3,2,1,0:T(8,128)(2,1)S(1)} async-done(((bf16[32,4,8,768]{3,2,1,0:T(8,128)(2,1)}), bf16[32,4,8,768]{3,2,1,0:T(8,128)(2,1)S(1)}, u32[]{:S(2)}, u32[]{:S(2)}) %all-to-all-start) | async-done | bytes 1572896 | tf_op jit(solution)/shard_map/all_to_all | solution.py:83
  240.1 2.8 fusion.20
  243.7 26.5 %all_to_all.35 = bf16[128,8,768]{2,1,0:T(8,128)(2,1)S(1)} all-to-all(bf16[128,8,768]{2,1,0:T(8,128)(2,1)S(1)} %copy.63), channel_id=1, replica_groups=mesh['member'=32,'mp'=4] {'member'}, dimensions={0} | all-to-all | bytes 3145728 | tf_op jit(solution)/shard_map/all_to_all | solution.py:126
  271.8 1.8 convolution_bitcast_fusion
  273.7 2.0 copy.69
  275.9 1.8 convolution_convert_fusion
  277.7 8.3 %fusion.46 = f32[2048,1024]{1,0:T(8,128)S(1)} fusion(bf16[1024,1024]{1,0:T(8,128)(2,1)S(1)} %convolution_convert_fusion, f32[2048,1024]{1,0:T(8,128)} %copy-done.14), kind=kOutput, calls=%fused_computation.128 | convolution fusion | flops 4313841664 | bytes 18874368 | tf_op jit(solution)/shard_map/dot_general | solution.py:47
  286.0 4.1 copy.68
  291.7 16.7 %fusion.10 = f32[2048,1024]{0,1:T(8,128)} fusion(bf16[1024,1024]{1,0:T(8,128)(2,1)S(1)} %bitcast.230, f32[2048,1024]{1,0:T(8,128)} %copy-done.14, bf16[1024,1024]{1,0:T(8,128)(2,1)} %copy-done.13, bf16[2048,1024]{1,0:T(8,128)(2,1)} %reshape_reshape.3), kind=kOutput, calls=%fused_computation.17 | convolution fusion | flops 8631877632 | bytes 25165824 | tf_op jit(solution)/shard_map/dot_general | solution.py:47
  308.4 7.8 %copy.67 = f32[32,4,8,2048]{3,2,0,1:T(8,128)} copy(f32[32,4,8,2048]{3,2,1,0:T(8,128)} %bitcast.220) | data formatting | bytes 16777216 | tf_op jit(solution)/shard_map/reshape | solution.py:58
  316.2 17.8 %all_to_all.36 = f32[32,8,768]{2,1,0:T(8,128)S(1)} all-to-all(f32[32,8,768]{2,1,0:T(8,128)} %bitcast.271), channel_id=1, replica_groups=mesh['member'=32,'mp'=4] {'member'}, dimensions={0} | all-to-all | bytes 1572864 | tf_op jit(solution)/shard_map/all_to_all | solution.py:18
  334.1 59.7 %reduce-scatter.6.cloned.1.call-done = f32[512,1024]{1,0:T(8,128)} async-done(((f32[2048,1024]{1,0:T(8,128)}), f32[512,1024]{1,0:T(8,128)}) %reduce-scatter.6.cloned.1.call-update) | async-done | bytes 2097168 | tf_op jit(solution)/shard_map/reduce_scatter | solution.py:62
  393.8 7.6 %all-to-all-start.3 = ((f32[32,16,1024]{2,1,0:T(8,128)}), f32[32,16,1024]{2,1,0:T(8,128)S(1)}, u32[]{:S(2)}, u32[]{:S(2)}) async-start(f32[32,16,1024]{2,1,0:T(8,128)} %bitcast.232), calls=%async_computation.5 | async-start | bytes 4194304 | tf_op jit(solution)/shard_map/all_to_all | solution.py:18
  401.4 75.0 %reduce-scatter.4.cloned.1.call-done = f32[256,2048]{1,0:T(8,128)} async-done(((f32[1024,2048]{1,0:T(8,128)}), f32[256,2048]{1,0:T(8,128)}) %reduce-scatter.4.cloned.1.call-update) | async-done | bytes 2097168 | tf_op jit(solution)/shard_map/reduce_scatter | solution.py:62
  476.4 7.7 %all-to-all-start.2 = ((f32[32,8,2048]{2,1,0:T(8,128)}), f32[32,8,2048]{2,1,0:T(8,128)}, u32[]{:S(2)}, u32[]{:S(2)}) async-start(f32[32,8,2048]{2,1,0:T(8,128)} %bitcast.231), calls=%async_computation.3 | async-start | bytes 4194304 | tf_op jit(solution)/shard_map/all_to_all | solution.py:18
  484.1 81.5 %all-reduce = (f32[]{:T(128)}, f32[]{:T(128)}) all-reduce(f32[]{:T(128)} %get-tuple-element.9, f32[]{:T(128)} %get-tuple-element.8), channel_id=1, replica_groups=mesh['member'=32,'mp'=4] {'member','mp'}, use_global_device_ids=true, to_apply=%region_6.7 | all-reduce | flops 2 | bytes 16 | tf_op jit(solution)/shard_map/psum | solution.py:125
  568.3 1.7 reduce_sum.96
  (96 shorter events, 33.7 us)
Async XLA Ops:
  7.2 207.8 %copy-start = (f32[8,768]{1,0:T(8,128)S(1)}, f32[8,768]{1,0:T(8,128)}, u32[]{:S(2)}) copy-start(f32[8,768]{1,0:T(8,128)} %param.11) | copy-start | bytes 73732
  7.2 2.0 copy-start.7
  7.2 2.5 copy-start.8
  7.2 116.6 %all-gather.3.cloned.1.call-start = ((), (), s32[]{:S(2)}) async-start(), calls=%async_computation.11 | async-start | bytes 12451840 | tf_op jit(solution)/shard_map/all_gather | solution.py:30
  24.0 1.6 copy-start.3
  158.4 6.4 %slice-start = ((bf16[4,1245184]{1,0:T(4,128)(2,1)}), bf16[4,196608]{1,0:T(4,128)(2,1)S(1)}, s32[]{:S(2)}) async-start(bf16[4,1245184]{1,0:T(4,128)(2,1)} %reshape.134), calls=%async_computation.12 | async-start | bytes 3145728 | tf_op jit(solution)/shard_map/slice | solution.py:32
  173.1 7.2 %copy-start.2 = (bf16[2048,1024]{1,0:T(8,128)(2,1)S(1)}, bf16[2048,1024]{1,0:T(8,128)(2,1)}, u32[]{:S(2)}) copy-start(bf16[2048,1024]{1,0:T(8,128)(2,1)} %reshape_reshape.3) | copy-start | bytes 12582916
  173.1 7.2 %copy-start.5 = (bf16[1024,1024]{0,1:T(8,128)(2,1)S(1)}, bf16[1024,1024]{0,1:T(8,128)(2,1)}, u32[]{:S(2)}) copy-start(bf16[1024,1024]{0,1:T(8,128)(2,1)} %copy.75) | copy-start | bytes 6291460
  180.2 5.2 copy-start.14
  180.3 5.2 copy-start.6
  185.5 1.9 copy-start.11
  201.0 13.9 %copy-start.9 = (s32[8]{0:T(128)S(1)}, s32[8]{0:T(128)}, u32[]{:S(2)}) copy-start(s32[8]{0:T(128)} %param.12) | copy-start | bytes 100
  207.2 30.3 %all-to-all-start = ((bf16[32,4,8,768]{3,2,1,0:T(8,128)(2,1)}), bf16[32,4,8,768]{3,2,1,0:T(8,128)(2,1)S(1)}, u32[]{:S(2)}, u32[]{:S(2)}) async-start(bf16[32,4,8,768]{3,2,1,0:T(8,128)(2,1)} %constant_dynamic-update-slice_fusion), calls=%async_computation | async-start | bytes 3145728 | tf_op jit(solution)/shard_map/all_to_all | solution.py:83
  214.9 101.4 %reduce-scatter.8.cloned.1.call-start = ((), (), s32[]{:S(2)}) async-start(), calls=%async_computation.10 | async-start | bytes 3932160 | tf_op jit(solution)/shard_map/reduce_scatter | solution.py:62
  238.5 0.9 copy-start.10
  270.2 1.6 copy-start.12
  275.7 118.1 %reduce-scatter.6.cloned.1.call-start = ((), (), s32[]{:S(2)}) async-start(), calls=%async_computation.9 | async-start | bytes 10485760 | tf_op jit(solution)/shard_map/reduce_scatter | solution.py:62
  277.7 8.3 %copy-start.13 = (bf16[1024,1024]{1,0:T(8,128)(2,1)}, bf16[1024,1024]{1,0:T(8,128)(2,1)S(1)}, u32[]{:S(2)}) copy-start(bf16[1024,1024]{1,0:T(8,128)(2,1)S(1)} %convolution_convert_fusion) | copy-start | bytes 6291460
  290.1 1.6 copy-start.4
  290.1 186.3 %reduce-scatter.4.cloned.1.call-start = ((), (), s32[]{:S(2)}) async-start(), calls=%async_computation.8 | async-start | bytes 10485760 | tf_op jit(solution)/shard_map/reduce_scatter | solution.py:62
  393.8 82.6 %all-to-all-start.3 = ((f32[32,16,1024]{2,1,0:T(8,128)}), f32[32,16,1024]{2,1,0:T(8,128)S(1)}, u32[]{:S(2)}, u32[]{:S(2)}) async-start(f32[32,16,1024]{2,1,0:T(8,128)} %bitcast.232), calls=%async_computation.5 | async-start | bytes 4194304 | tf_op jit(solution)/shard_map/all_to_all | solution.py:18
  476.4 91.9 %all-to-all-start.2 = ((f32[32,8,2048]{2,1,0:T(8,128)}), f32[32,8,2048]{2,1,0:T(8,128)}, u32[]{:S(2)}, u32[]{:S(2)}) async-start(f32[32,8,2048]{2,1,0:T(8,128)} %bitcast.231), calls=%async_computation.3 | async-start | bytes 4194304 | tf_op jit(solution)/shard_map/all_to_all | solution.py:18
  567.0 3.7 copy-start.1
Sparse Core Ops, SparseCore 0:
  24.1 99.6 all-gather.2
  275.8 35.2 reduce-scatter.7
  313.6 80.1 reduce-scatter.5
  396.1 80.2 reduce-scatter.3
